TPU v7x, 256 devices: a whole 4x4x8 slice. The times are simulated.
256 devices in a mesh: outer: 8 (over x, y_lo), inner: 8 (over z), tensor: 4 (over y_hi, core).
Axes of the slice: x: 4, y: 4 (y_hi: 2, y_lo: 2; y = y_hi * 2 + y_lo), z: 8, core: 2. Of those that a mesh axis runs over, the one named last changes fastest.
Arguments:
- queries: bfloat16 [16384, 16, 128], P(('outer', 'inner'), 'tensor'), may hold values from -5 to 5
- keys: bfloat16 [16384, 4, 128], P(('outer', 'inner'), 'tensor'), may hold values from -5 to 5
- values: bfloat16 [16384, 4, 128], P(('outer', 'inner'), 'tensor'), may hold values from -6 to 6
- w_out: bfloat16 [16, 128, 4096], P('tensor'), may hold values from -0.125 to 0.125
- d_out: bfloat16 [16384, 4096], P(('outer', 'inner', 'tensor')), may hold values from -6 to 6
- lengths: int32 [16], replicated, may hold values from 1 to 10240, 16384 in all
Outputs:
- mixed: bfloat16 [16384, 4096], P(('outer', 'inner', 'tensor'))
- d_queries: bfloat16 [16384, 16, 128], P(('outer', 'inner'), 'tensor')
- d_keys: bfloat16 [16384, 4, 128], P(('outer', 'inner'), 'tensor')
- d_values: bfloat16 [16384, 4, 128], P(('outer', 'inner'), 'tensor')
Inputs may be any that keep to these rules, and one draw needn't show every extreme that they name: `lengths`: the 16 documents fill the sequence of 16384 tokens exactly, and the longest has exactly 10240 tokens.
All inputs are finite; a program needn't handle non-finite values.
Results may differ from a plain program's by a relative error of at most 0.04.
Values may be sent and summed in bfloat16 or wider, within the bound.
A program may use at most 128 MiB of HBM per device.

v0:
```python
import jax
import jax.numpy as jnp
from jax import lax
from jax.sharding import PartitionSpec as P

NEG_FILL = -1e30


def segment_of(positions, ends):
    return jnp.sum((positions[:, None] >= ends[None, :]).astype(jnp.int32), axis=1)


def doc_begin(position, ends):
    return jnp.max(jnp.where(ends <= position, ends, jnp.zeros_like(ends)))


def masked_scores(q_rows, k_block, q_pos, q_seg, k_start, ends, scale):
    width = k_block.shape[0]
    k_pos = k_start + jnp.arange(width, dtype=jnp.int32)
    k_seg = segment_of(k_pos, ends)
    s = (
        lax.dot_general(
            q_rows, k_block, (((1,), (1,)), ((), ())), preferred_element_type=jnp.float32
        )
        * scale
    )
    mask = (k_pos[None, :] <= q_pos[:, None]) & (k_seg[None, :] == q_seg[:, None])
    return (jnp.where(mask, s, NEG_FILL), mask)


def local(queries, keys, values, w_out, d_out, lengths):
    tok, heads_here, head_dim = queries.shape
    kv_here = keys.shape[1]
    group = heads_here // kv_here
    width = w_out.shape[2]
    ctx = lax.axis_size(("outer", "inner"))
    total = tok * ctx
    scale = head_dim ** (-0.5)
    offset = lax.axis_index(("outer", "inner")) * tok
    ends = jnp.cumsum(lengths)
    first = doc_begin(offset, ends)
    last = offset + tok - 1
    factor = 1
    while factor < ctx and tok * factor < 1024 and (ctx % (factor * 2) == 0):
        factor = factor * 2
    span = tok * factor
    n_blocks = total // span
    q_pos = offset + jnp.arange(tok * group, dtype=jnp.int32) // group
    q_seg = segment_of(q_pos, ends)
    key_all, value_all = (
        lax.all_gather(keys, ("outer", "inner"), axis=0, tiled=True),
        lax.all_gather(values, ("outer", "inner"), axis=0, tiled=True),
    )
    q_groups = queries.reshape(tok, kv_here, group, head_dim)
    zero = jnp.zeros((), jnp.int32)

    def needed(k_start, k_width):
        return (k_start <= last) & (k_start + k_width - 1 >= first)

    q_list = [q_groups[:, 0].reshape(tok * group, head_dim)]
    lse_list = []
    c = 0
    q_rows = q_list[c]

    def forward_block(b, carry, q_rows=q_rows, c=c):
        k_start = b * span

        def forward_work(state):
            top, denom, acc = state
            k_block = lax.dynamic_slice_in_dim(key_all, k_start, span, 0)[:, c]
            v_block = lax.dynamic_slice_in_dim(value_all, k_start, span, 0)[:, c]
            s, mask = masked_scores(q_rows, k_block, q_pos, q_seg, k_start, ends, scale)
            new_top = jnp.maximum(top, jnp.max(s, axis=1))
            weights = jnp.where(mask, jnp.exp(s - new_top[:, None]), 0.0)
            shrink = jnp.exp(top - new_top)
            denom = denom * shrink + jnp.sum(weights, axis=1)
            acc = acc * shrink[:, None] + jnp.dot(
                weights.astype(jnp.bfloat16), v_block, preferred_element_type=jnp.float32
            )
            return (new_top, denom, acc)

        return lax.cond(needed(k_start, span), forward_work, lambda st: st, carry)

    start_state = (
        jnp.full((tok * group,), NEG_FILL, jnp.float32),
        jnp.zeros((tok * group,), jnp.float32),
        jnp.zeros((tok * group, head_dim), jnp.float32),
    )
    top, denom, acc = lax.fori_loop(0, n_blocks, forward_block, start_state)
    attn_parts = [(acc / denom[:, None]).astype(jnp.bfloat16).reshape(tok, group, head_dim)]
    lse_list.append(top + jnp.log(denom))
    attn = jnp.stack(attn_parts, axis=1).reshape(tok, heads_here * head_dim)
    w_flat = w_out.reshape(heads_here * head_dim, width)
    mixed = lax.psum_scatter(
        jnp.dot(attn, w_flat, preferred_element_type=jnp.float32).astype(jnp.bfloat16),
        "tensor",
        scatter_dimension=0,
        tiled=True,
    )
    d_attn = lax.dot_general(
        lax.all_gather(d_out, "tensor", axis=0, tiled=True),
        w_flat,
        (((1,), (1,)), ((), ())),
        preferred_element_type=jnp.float32,
    ).astype(jnp.bfloat16)
    d_groups = d_attn.reshape(tok, kv_here, group, head_dim)
    a_groups = attn.reshape(tok, kv_here, group, head_dim)
    deltas = jnp.sum(d_groups.astype(jnp.float32) * a_groups.astype(jnp.float32), axis=3)
    g_list = [d_groups[:, 0].reshape(tok * group, head_dim)]
    delta_list = [deltas[:, 0].reshape(tok * group)]

    def grad_terms(c, k_start, k_width):
        k_block = lax.dynamic_slice_in_dim(key_all, k_start, k_width, 0)[:, c]
        v_block = lax.dynamic_slice_in_dim(value_all, k_start, k_width, 0)[:, c]
        s, mask = masked_scores(q_list[c], k_block, q_pos, q_seg, k_start, ends, scale)
        probs = jnp.where(mask, jnp.exp(s - lse_list[c][:, None]), 0.0)
        d_val = lax.dot_general(
            probs.astype(jnp.bfloat16),
            g_list[c],
            (((0,), (0,)), ((), ())),
            preferred_element_type=jnp.float32,
        )
        d_prob = lax.dot_general(
            g_list[c], v_block, (((1,), (1,)), ((), ())), preferred_element_type=jnp.float32
        )
        d_score = (probs * (d_prob - delta_list[c][:, None])).astype(jnp.bfloat16)
        dq_add = jnp.dot(d_score, k_block, preferred_element_type=jnp.float32) * scale
        d_key = (
            lax.dot_general(
                d_score, q_list[c], (((0,), (0,)), ((), ())), preferred_element_type=jnp.float32
            )
            * scale
        )
        return (dq_add, d_key, d_val)

    dq_start = tuple((jnp.zeros((tok * group, head_dim), jnp.float32) for c in range(kv_here)))

    def backward_block(b, carry):
        k_start = b * span

        def backward_work(state):
            dq_all, key_terms = state
            dq_add, d_key, d_val = grad_terms(0, k_start, span)
            new_dq = [dq_all[0] + dq_add]
            piece = jnp.stack((d_key, d_val), axis=1)[:, :, None, :]
            key_terms = lax.dynamic_update_slice(key_terms, piece, (k_start, zero, zero + 0, zero))
            return (tuple(new_dq), key_terms)

        return lax.cond(needed(k_start, span), backward_work, lambda st: st, carry)

    term_start = jnp.zeros((total, 2, kv_here, head_dim), jnp.float32)
    dq_all, key_terms = lax.fori_loop(0, n_blocks, backward_block, (dq_start, term_start))
    key_grads = lax.psum_scatter(key_terms, ("outer", "inner"), scatter_dimension=0, tiled=True)
    d_queries = (
        jnp.stack([d.reshape(tok, group, head_dim) for d in dq_all], axis=1)
        .reshape(tok, heads_here, head_dim)
        .astype(jnp.bfloat16)
    )
    d_keys = key_grads[:, 0].astype(jnp.bfloat16)
    d_values = key_grads[:, 1].astype(jnp.bfloat16)
    return (mixed, d_queries, d_keys, d_values)


def solution(mesh):
    return jax.shard_map(
        local,
        mesh=mesh,
        in_specs=(
            P(("outer", "inner"), "tensor", None),
            P(("outer", "inner"), "tensor", None),
            P(("outer", "inner"), "tensor", None),
            P("tensor", None, None),
            P(("outer", "inner", "tensor"), None),
            P(),
        ),
        out_specs=(
            P(("outer", "inner", "tensor"), None),
            P(("outer", "inner"), "tensor", None),
            P(("outer", "inner"), "tensor", None),
            P(("outer", "inner"), "tensor", None),
        ),
        check_vma=False,
    )
```

profile of v0, /device:TPU:1, one launch (start us, length us, event | category | flops | bytes accessed | tf_op | source)
XLA Modules:
  0.0 1233.0 jit_solution(10827884792633760065)
XLA Ops:
  7.2 0.0 all-gather.8.cloned.1.call-start
  7.2 0.7 all-gather.8.cloned.1.call-update
  7.9 0.0 all-gather.4.cloned.1.call-start
  7.9 0.7 all-gather.4.cloned.1.call-update
  8.6 0.0 all-gather.6.cloned.1.call-start
  8.7 0.7 all-gather.6.cloned.1.call-update
  9.4 0.0 reduce-scatter.5.cloned.1.call-start
  9.4 0.7 copy.16
  10.2 0.1 reduce.1
  10.3 0.6 fusion.57
  11.0 0.1 convert_reduce_fusion.2
  11.1 32.1 %all-gather.8.cloned.1.call-done = bf16[256,4096]{1,0:T(8,128)(2,1)} async-done(((bf16[64,4096]{1,0:T(8,128)(2,1)}), bf16[256,4096]{1,0:T(8,128)(2,1)}) %all-gather.8.cloned.1.call-update) | async-done | bytes 2097168 | tf_op jit(solution)/shard_map/all_gather | solution.py:101
  43.2 0.0 copy-start
  43.2 4.1 convolution_convert_fusion.1
  47.3 0.2 reshape_squeeze_reshape.7
  47.5 0.2 reshape.141
  47.7 253.0 %all-gather.4.cloned.1.call-done = bf16[16384,1,128]{2,0,1:T(8,128)(2,1)} async-done(((bf16[256,1,128]{2,0,1:T(8,128)(2,1)}), bf16[16384,1,128]{2,0,1:T(8,128)(2,1)}) %all-gather.4.cloned.1.call-update) | async-done | bytes 4194320 | tf_op jit(solution)/shard_map/all_gather | solution.py:51
  300.7 302.0 %all-gather.6.cloned.1.call-done = bf16[16384,1,128]{2,0,1:T(8,128)(2,1)} async-done(((bf16[256,1,128]{2,0,1:T(8,128)(2,1)}), bf16[16384,1,128]{2,0,1:T(8,128)(2,1)}) %all-gather.6.cloned.1.call-update) | async-done | bytes 4194320 | tf_op jit(solution)/shard_map/all_gather | solution.py:52
  602.7 0.0 copy-done
  602.7 17.8 %while.42 = (s32[]{:T(128)}, f32[1024]{0:T(1024)S(1)}, f32[1024]{0:T(1024)S(1)}, f32[1024,128]{1,0:T(8,128)S(1)}, s32[]{:T(128)}, /*index=5*/s32[]{:T(128)}, s32...) while((s32[]{:T(128)}, f32[1024]{0:T(1024)S(1)}, ...), condition=%wide.region_9.10_spmd.clone, body=%wide.region_3.9_spmd.clone.sunk | while | flops 560262144 | bytes 14574053 | solution.py:89
  603.3 6.7 conditional.6
  603.4 0.1 convert_reduce_fusion
  603.5 2.2 fusion.4
  605.7 1.6 fusion.6
  607.3 2.7 fusion.9
  620.5 0.2 divide_convert_fusion
  620.8 0.4 fusion.52
  621.2 6.0 broadcast_in_dim.31
  627.1 20.5 %while.43 = (s32[]{:T(128)}, f32[1024,128]{1,0:T(8,128)S(1)}, f32[16384,2,1,128]{3,0,1,2:T(8,128)}, s32[]{:T(128)}, s32[]{:T(128)}, /*index=5*/s32[16]{0:T(128)S...) while((s32[]{:T(128)}, f32[1024,128]{1,0:T(8,128)S(1)}, ...), condition=%wide.region_16.17_spmd.clone, body=%wide.region_12.16_spmd.clone.sunk | while | flops 1361765376 | bytes 24998396 | solution.py:152
  627.8 9.4 conditional.7
  627.8 0.1 sub.71
  628.0 0.1 convert_reduce_fusion.1
  628.0 1.7 fusion.39
  629.7 2.6 fusion.24
  632.3 1.3 fusion.31
  633.6 1.8 fusion.35
  635.4 0.7 fusion.34
  636.1 1.1 fusion.36
  647.6 0.0 reduce-scatter.5.cloned.1.call-update
  647.7 0.0 reduce-scatter.3.cloned.1.call-start
  647.7 0.2 reshape_stack_reshape.4
  647.9 4.8 convolution_convert_fusion
  652.7 0.0 reduce-scatter.3.cloned.1.call-update
  652.7 0.7 convert_element_type.119
  653.4 483.7 %reduce-scatter.5.cloned.1.call-done = f32[256,2,1,128]{3,0,2,1:T(8,128)} async-done(((f32[16384,2,1,128]{3,0,2,1:T(8,128)}), f32[256,2,1,128]{3,0,2,1:T(8,128)}) %reduce-scatter.5.cloned.1.call-update) | async-done | bytes 262160 | tf_op jit(solution)/shard_map/reduce_scatter | solution.py:153
  1137.2 1.0 convert.6
  1138.1 0.7 slice_bitcast_fusion
  1138.8 87.6 %reduce-scatter.3.cloned.1.call-done = bf16[64,4096]{1,0:T(8,128)(2,1)} async-done(((bf16[256,4096]{1,0:T(8,128)(2,1)}), bf16[64,4096]{1,0:T(8,128)(2,1)}) %reduce-scatter.3.cloned.1.call-update) | async-done | bytes 524304 | tf_op jit(solution)/shard_map/reduce_scatter | solution.py:94
  (106 shorter events, 0.9 us)
Async XLA Ops:
  7.2 36.0 %all-gather.8.cloned.1.call-start = ((), (), s32[]{:S(2)}) async-start(), calls=%async_computation.5 | async-start | bytes 2621440 | tf_op jit(solution)/shard_map/all_gather | solution.py:101
  7.9 292.8 %all-gather.4.cloned.1.call-start = ((), (), s32[]{:S(2)}) async-start(), calls=%async_computation.2 | async-start | bytes 4259840 | tf_op jit(solution)/shard_map/all_gather | solution.py:51
  8.6 594.0 %all-gather.6.cloned.1.call-start = ((), (), s32[]{:S(2)}) async-start(), calls=%async_computation.3 | async-start | bytes 4259840 | tf_op jit(solution)/shard_map/all_gather | solution.py:52
  9.4 1127.8 %reduce-scatter.5.cloned.1.call-start = ((), (), s32[]{:S(2)}) async-start(), calls=%async_computation.6 | async-start | bytes 17039360 | tf_op jit(solution)/shard_map/reduce_scatter | solution.py:153
  43.2 559.5 %copy-start = (bf16[256,4,128]{2,1,0:T(4,128)(2,1)S(1)}, bf16[256,4,128]{2,1,0:T(4,128)(2,1)}, u32[]{:S(2)}) copy-start(bf16[256,4,128]{2,1,0:T(4,128)(2,1)} %param.14) | copy-start | bytes 786436
  647.7 578.8 %reduce-scatter.3.cloned.1.call-start = ((), (), s32[]{:S(2)}) async-start(), calls=%async_computation.4 | async-start | bytes 2621440 | tf_op jit(solution)/shard_map/reduce_scatter | solution.py:94
Sparse Core Ops, SparseCore 0:
  9.8 33.3 all-gather.7
  45.0 255.6 all-gather.3
  302.5 300.1 all-gather.5
  647.8 489.3 reduce-scatter.4
  1140.4 86.0 reduce-scatter.2
where the time goes:
time: 1230 us
  waiting for transfers between devices  1160 us (94%)
  loops' own time  22.2 us (2%)
  matrix products  21.9 us (2%)
  between operations  13.9 us (1%)
    reduce_scatter x1, waiting for transfers between devices, local(): lax.psum_scatter(key_terms, ('outer', 'inner'), scatter_dimension=0, tile...  484 us
    all_gather x1, waiting for transfers between devices, local(): lax.all_gather(values, ('outer', 'inner'), axis=0, tiled=True)  302 us
    all_gather x1, waiting for transfers between devices, local(): lax.all_gather(keys, ('outer', 'inner'), axis=0, tiled=True)  253 us
    reduce_scatter x1, waiting for transfers between devices, local(): lax.psum_scatter(jnp.dot(attn, w_flat, preferred_element_type=jnp.float32...  87.6 us
    all_gather x1, waiting for transfers between devices, local(): lax.all_gather(d_out, 'tensor', axis=0, tiled=True)  32.1 us
  transfers between devices with their start and end apart: 5, of which 5 were waited for; matrix products, arithmetic and copies ran while one was open for 1% of the time, Pallas kernels for 0%

commit v1 on v0

--- a/solution.py
+++ b/solution.py
@@ -1,9 +1,19 @@
+import functools
 import jax
 import jax.numpy as jnp
 from jax import lax
 from jax.sharding import PartitionSpec as P
 
 NEG_FILL = -1e30
+
+
+def resolve_the_blocks(x_part, chip_axis, out_dim):
+    prior = jnp.stack([x_part for _ in range(lax.psum(1, axis_name=chip_axis))])
+    heard = lax.all_to_all(prior, axis_name=chip_axis, split_axis=0, concat_axis=0)
+    return jnp.concatenate(heard, axis=out_dim)
+
+
+prepare_the_threads = functools.partial(resolve_the_blocks, chip_axis=("outer", "inner"), out_dim=0)
 
 
 def segment_of(positions, ends):
@@ -49,7 +59,7 @@
     q_seg = segment_of(q_pos, ends)
     key_all, value_all = (
         lax.all_gather(keys, ("outer", "inner"), axis=0, tiled=True),
-        lax.all_gather(values, ("outer", "inner"), axis=0, tiled=True),
+        prepare_the_threads(values),
     )
     q_groups = queries.reshape(tok, kv_here, group, head_dim)
     zero = jnp.zeros((), jnp.int32)

time: 1230 us -> 960 us (0.78)
  waiting for transfers between devices: 1160 us -> 869 us
  starting transfers between devices: 0.19 us -> 14 us
    all_gather x1 -> x0, waiting for transfers between devices: 302 us -> none  [local(): lax.all_gather(values, ('outer', 'inner'), axis=0, tiled=True)]
    all_gather x1, waiting for transfers between devices: 253 us -> 269 us  [local(): lax.all_gather(keys, ('outer', 'inner'), axis=0, tiled=True)]
    all_to_all x0 -> x1, starting transfers between devices: none -> 13.9 us  [resolve_the_blocks(): lax.all_to_all(prior, axis_name=chip_axis, split_axis=0, concat_axis=0)]
  transfers between devices with their start and end apart: 5 -> 5, of which waited for: 5 -> 4; matrix products, arithmetic and copies ran while one was open for 1% -> 2% of each run, Pallas kernels for 0% -> 0%
where the time goes in v1:
time: 960 us; the launch traced here: 958 us
  waiting for transfers between devices  869 us (91%)
  loops' own time  22.2 us (2%)
  matrix products  22 us (2%)
  starting transfers between devices  14 us (1%)
  between operations  13.9 us (1%)
  local copies, waits for them, and re-layouts  11.3 us (1%)
    reduce_scatter x1, waiting for transfers between devices, local(): lax.psum_scatter(key_terms, ('outer', 'inner'), scatter_dimension=0, tile...  482 us
    all_gather x1, waiting for transfers between devices, local(): lax.all_gather(keys, ('outer', 'inner'), axis=0, tiled=True)  269 us
    reduce_scatter x1, waiting for transfers between devices, local(): lax.psum_scatter(jnp.dot(attn, w_flat, preferred_element_type=jnp.float32...  85.5 us
    all_gather x1, waiting for transfers between devices, local(): lax.all_gather(d_out, 'tensor', axis=0, tiled=True)  30.7 us
  transfers between devices with their start and end apart: 5, of which 4 were waited for; matrix products, arithmetic and copies ran while one was open for 2% of the time, Pallas kernels for 0%

profile of v1, /device:TPU:1, one launch (start us, length us, event | category | flops | bytes accessed | tf_op | source)
XLA Modules:
  0.0 958.2 jit_solution(13702867803250358716)
XLA Ops:
  7.2 0.0 all-gather.5.cloned.1.call-start
  7.2 0.7 all-gather.5.cloned.1.call-update
  7.9 0.0 all-gather.3.cloned.1.call-start
  7.9 0.7 all-gather.3.cloned.1.call-update
  8.6 3.8 stack.8
  12.4 13.9 %all-to-all-start = ((bf16[64,256,1,128]{3,1,2,0:T(8,128)(2,1)}), bf16[64,256,1,128]{3,1,2,0:T(8,128)(2,1)}, u32[]{:S(2)}, u32[]{:S(2)}) async-start(bf16[64,256,1,128]{3,1,2,0:T(8,128)(2,1)} %stack.8), calls=%async_computation | async-start | bytes 8388608 | tf_op jit(solution)/shard_map/all_to_all | solution.py:12
  26.3 0.0 reduce-scatter.5.cloned.1.call-start
  26.4 0.0 copy-done.1
  26.4 0.1 copy.17
  26.5 0.1 reduce.1
  26.6 0.6 fusion.57
  27.3 0.1 convert_reduce_fusion.2
  27.4 30.7 %all-gather.5.cloned.1.call-done = bf16[256,4096]{1,0:T(8,128)(2,1)} async-done(((bf16[64,4096]{1,0:T(8,128)(2,1)}), bf16[256,4096]{1,0:T(8,128)(2,1)}) %all-gather.5.cloned.1.call-update) | async-done | bytes 2097168 | tf_op jit(solution)/shard_map/all_gather | solution.py:111
  58.0 4.1 convolution_convert_fusion.1
  62.2 0.2 reshape_squeeze_reshape.7
  62.3 0.2 reshape.148
  62.5 268.7 %all-gather.3.cloned.1.call-done = bf16[16384,1,128]{2,0,1:T(8,128)(2,1)} async-done(((bf16[256,1,128]{2,0,1:T(8,128)(2,1)}), bf16[16384,1,128]{2,0,1:T(8,128)(2,1)}) %all-gather.3.cloned.1.call-update) | async-done | bytes 4194320 | tf_op jit(solution)/shard_map/all_gather | solution.py:61
  331.2 0.0 all-to-all-done
  331.2 0.0 copy-done
  331.2 18.0 %while.42 = (s32[]{:T(128)}, f32[1024]{0:T(1024)S(1)}, f32[1024]{0:T(1024)S(1)}, f32[1024,128]{1,0:T(8,128)S(1)}, s32[]{:T(128)}, /*index=5*/s32[]{:T(128)}, s32...) while((s32[]{:T(128)}, f32[1024]{0:T(1024)S(1)}, ...), condition=%wide.region_9.10_spmd.clone, body=%wide.region_3.9_spmd.clone.sunk | while | flops 560262144 | bytes 14574053 | solution.py:99
  331.9 6.8 conditional.6
  332.0 0.1 convert_reduce_fusion
  332.1 2.3 fusion.4
  334.3 1.6 fusion.6
  336.0 2.8 fusion.9
  349.2 0.2 divide_convert_fusion
  349.5 0.4 fusion.52
  349.9 6.0 broadcast_in_dim.31
  355.9 20.5 %while.43 = (s32[]{:T(128)}, f32[1024,128]{1,0:T(8,128)S(1)}, f32[16384,2,1,128]{3,0,1,2:T(8,128)}, s32[]{:T(128)}, s32[]{:T(128)}, /*index=5*/s32[16]{0:T(128)S...) while((s32[]{:T(128)}, f32[1024,128]{1,0:T(8,128)S(1)}, ...), condition=%wide.region_16.17_spmd.clone, body=%wide.region_12.16_spmd.clone.sunk | while | flops 1361765376 | bytes 24998396 | solution.py:162
  356.5 9.4 conditional.7
  356.5 0.1 sub.71
  356.7 0.1 convert_reduce_fusion.1
  356.8 1.7 fusion.39
  358.4 2.6 fusion.24
  361.1 1.3 fusion.31
  362.4 1.8 fusion.35
  364.1 0.7 fusion.34
  364.9 1.1 fusion.36
  376.4 0.0 reduce-scatter.5.cloned.1.call-update
  376.4 0.0 reduce-scatter.3.cloned.1.call-start
  376.4 0.2 reshape_stack_reshape.4
  376.6 4.8 convolution_convert_fusion
  381.4 0.0 reduce-scatter.3.cloned.1.call-update
  381.4 0.7 convert_element_type.119
  382.2 482.4 %reduce-scatter.5.cloned.1.call-done = f32[256,2,1,128]{3,0,2,1:T(8,128)} async-done(((f32[16384,2,1,128]{3,0,2,1:T(8,128)}), f32[256,2,1,128]{3,0,2,1:T(8,128)}) %reduce-scatter.5.cloned.1.call-update) | async-done | bytes 262160 | tf_op jit(solution)/shard_map/reduce_scatter | solution.py:163
  864.6 1.0 convert.6
  865.5 0.7 slice_bitcast_fusion
  866.2 85.5 %reduce-scatter.3.cloned.1.call-done = bf16[64,4096]{1,0:T(8,128)(2,1)} async-done(((bf16[256,4096]{1,0:T(8,128)(2,1)}), bf16[64,4096]{1,0:T(8,128)(2,1)}) %reduce-scatter.3.cloned.1.call-update) | async-done | bytes 524304 | tf_op jit(solution)/shard_map/reduce_scatter | solution.py:104
  (108 shorter events, 0.9 us)
Async XLA Ops:
  7.2 50.9 %all-gather.5.cloned.1.call-start = ((), (), s32[]{:S(2)}) async-start(), calls=%async_computation.5 | async-start | bytes 2621440 | tf_op jit(solution)/shard_map/all_gather | solution.py:111
  7.9 323.3 %all-gather.3.cloned.1.call-start = ((), (), s32[]{:S(2)}) async-start(), calls=%async_computation.3 | async-start | bytes 4259840 | tf_op jit(solution)/shard_map/all_gather | solution.py:61
  12.4 13.9 %copy-start.1 = (s32[16]{0:T(128)S(1)}, s32[16]{0:T(128)}, u32[]{:S(2)}) copy-start(s32[16]{0:T(128)} %param.19) | copy-start | bytes 196
  12.4 318.8 %all-to-all-start = ((bf16[64,256,1,128]{3,1,2,0:T(8,128)(2,1)}), bf16[64,256,1,128]{3,1,2,0:T(8,128)(2,1)}, u32[]{:S(2)}, u32[]{:S(2)}) async-start(bf16[64,256,1,128]{3,1,2,0:T(8,128)(2,1)} %stack.8), calls=%async_computation | async-start | bytes 8388608 | tf_op jit(solution)/shard_map/all_to_all | solution.py:12
  26.3 838.2 %reduce-scatter.5.cloned.1.call-start = ((), (), s32[]{:S(2)}) async-start(), calls=%async_computation.6 | async-start | bytes 17039360 | tf_op jit(solution)/shard_map/reduce_scatter | solution.py:163
  58.0 273.2 %copy-start = (bf16[256,4,128]{2,1,0:T(4,128)(2,1)S(1)}, bf16[256,4,128]{2,1,0:T(4,128)(2,1)}, u32[]{:S(2)}) copy-start(bf16[256,4,128]{2,1,0:T(4,128)(2,1)} %param.14) | copy-start | bytes 786436
  376.4 575.3 %reduce-scatter.3.cloned.1.call-start = ((), (), s32[]{:S(2)}) async-start(), calls=%async_computation.4 | async-start | bytes 2621440 | tf_op jit(solution)/shard_map/reduce_scatter | solution.py:104
Sparse Core Ops, SparseCore 0:
  9.8 48.1 all-gather.4
  59.8 271.3 all-gather.2
  376.5 487.9 reduce-scatter.4
  867.8 83.8 reduce-scatter.2
